TPU v7x, 512 devices: a whole 4x4x16 slice. The times are simulated.
512 devices in a mesh: gy: 16 (over x_hi, y, core), gx: 32 (over z, x_lo).
Axes of the slice: x: 4 (x_hi: 2, x_lo: 2; x = x_hi * 2 + x_lo), y: 4, z: 16, core: 2. Of those that a mesh axis runs over, the one named last changes fastest.
Arguments:
- embeddings: bfloat16 [128, 4096, 128], P('gy', 'gx'), may hold values from -180 to 180
- affinity: float32 [4, 128, 4096], P(None, 'gy', 'gx'), may hold values from 0 to 1, as said below
- assignment: int32 [128, 4096], P('gy', 'gx'), may hold values from 0 to 1023
Outputs:
- min_distance: float32 [128, 4096], P('gy', 'gx')
- new_centroids: float32 [1024, 128], replicated
Inputs may be any that keep to these rules, and one draw needn't show every extreme that they name: `affinity`: weight 0 exactly for edges that leave the slab; every other edge weighs 0.05 or more.
All inputs are finite; a program needn't handle non-finite values.
Results may differ from a plain program's by a relative error of at most 0.00045.
Values may be sent and summed in bfloat16 or wider, within the bound.
No kernel may reach another device: no remote copies, remote signals or barrier semaphores. Data moves between devices by JAX's collectives and lax.ppermute only.
A program may use at most 64 MiB of HBM per device.

v0:
```python
import math
import jax
import jax.numpy as jnp
from jax import lax
from jax.sharding import PartitionSpec as P

K = 1024
DEGREE = 4
COEFFS = (0.5, 0.45, 0.35, 0.25, 0.15)


def extended(block, sides, width):
    for axis, dim in sides:
        count = lax.axis_size(axis)
        forward = [(i, i + 1) for i in range(count - 1)]
        backward = [(target, source) for source, target in forward]
        low = lax.ppermute(
            lax.slice_in_dim(block, block.shape[dim] - width, None, axis=dim), axis, forward
        )
        high = lax.ppermute(lax.slice_in_dim(block, 0, width, axis=dim), axis, backward)
        block = jnp.concatenate([low, block, high], axis=dim)
    return block


def degree_of(w_ext):
    w_east, w_south, w_diag, w_anti = (w_ext[0], w_ext[1], w_ext[2], w_ext[3])
    result = w_east[1:-1, 1:-1] + w_east[1:-1, :-2]
    result = result + w_south[1:-1, 1:-1] + w_south[:-2, 1:-1]
    result = result + w_diag[1:-1, 1:-1] + w_diag[:-2, :-2]
    return result + w_anti[1:-1, 1:-1] + w_anti[:-2, 2:]


def edge_sum(w_ext, field):
    w_east, w_south, w_diag, w_anti = (w_ext[0], w_ext[1], w_ext[2], w_ext[3])
    result = w_east[1:-1, 1:-1, None] * field[1:-1, 2:]
    result = result + w_east[1:-1, :-2, None] * field[1:-1, :-2]
    result = result + w_south[1:-1, 1:-1, None] * field[2:, 1:-1]
    result = result + w_south[:-2, 1:-1, None] * field[:-2, 1:-1]
    result = result + w_diag[1:-1, 1:-1, None] * field[2:, 2:]
    result = result + w_diag[:-2, :-2, None] * field[:-2, :-2]
    result = result + w_anti[1:-1, 1:-1, None] * field[2:, :-2]
    return result + w_anti[:-2, 2:, None] * field[:-2, 2:]


def whitening(gram, count):
    lower = jnp.linalg.cholesky(gram)
    identity = jnp.eye(gram.shape[0], dtype=gram.dtype)
    inverse = jax.scipy.linalg.solve_triangular(lower, identity, lower=True)
    return math.sqrt(count) * inverse.T


def on_device(embeddings, affinity, assignment):
    rows, cols, chans = embeddings.shape
    reach_all = DEGREE
    w_width = 1
    w_ext = extended(affinity, (("gy", 1), ("gx", 2)), w_width)
    scale = lax.rsqrt(degree_of(w_ext))[..., None]

    def apply_each(field):
        padded = extended(scale * field, (("gy", 0), ("gx", 1)), 1)
        return scale * edge_sum(w_ext, padded)

    previous = embeddings.astype(jnp.float32)
    current = apply_each(previous)
    filtered = COEFFS[0] * previous + COEFFS[1] * current
    for order in range(2, reach_all + 1):
        following = 2.0 * apply_each(current) - previous
        previous, current = (current, following)
        filtered = filtered + COEFFS[order] * following
    pixels = rows * cols
    flat = filtered.reshape(pixels, chans)
    labels = assignment.reshape(pixels)
    total_pixels = pixels * lax.axis_size("gy") * lax.axis_size("gx")
    clusters = K
    block = 128
    highest = lax.Precision.HIGHEST
    gram_local = lax.dot_general(
        flat, flat, (((0,), (0,)), ((), ())), precision=highest, preferred_element_type=jnp.float32
    )
    gram = lax.psum(gram_local, ("gy", "gx"))
    transform = whitening(gram, total_pixels)
    whitened = jnp.dot(flat, transform, precision=highest, preferred_element_type=jnp.float32)

    def one_block(index):
        first = index * block
        onehot = (labels[:, None] == first + jnp.arange(block, dtype=jnp.int32)[None, :]).astype(
            jnp.float32
        )
        partial_sums = lax.dot_general(
            onehot,
            whitened,
            (((0,), (0,)), ((), ())),
            precision=highest,
            preferred_element_type=jnp.float32,
        )
        return (partial_sums, jnp.sum(onehot, axis=0))

    block_sums, block_counts = lax.map(one_block, jnp.arange(clusters // block, dtype=jnp.int32))
    local_sums = block_sums.reshape(clusters, chans)
    local_counts = block_counts.reshape(clusters)
    sums, counts = lax.psum((local_sums, local_counts), ("gy", "gx"))
    centroids = sums / (counts + 1.0)[:, None]
    norms = jnp.sum(whitened * whitened, axis=1)

    def nearest(index, best):
        centre_part = lax.dynamic_slice_in_dim(centroids, index * block, block, 0)
        cross = lax.dot_general(
            whitened,
            centre_part,
            (((1,), (1,)), ((), ())),
            precision=highest,
            preferred_element_type=jnp.float32,
        )
        part_norms = jnp.sum(centre_part * centre_part, axis=1)
        distance = (norms[:, None] - 2.0 * cross + part_norms[None, :]) / chans
        return jnp.minimum(best, jnp.min(distance, axis=1))

    best = lax.fori_loop(0, clusters // block, nearest, jnp.full((pixels,), jnp.inf, jnp.float32))
    return (best.reshape(rows, cols), centroids)


def solution(mesh):
    return jax.shard_map(
        on_device,
        mesh=mesh,
        in_specs=(P("gy", "gx", None), P(None, "gy", "gx"), P("gy", "gx")),
        out_specs=(P("gy", "gx"), P()),
        check_vma=False,
    )
```

profile of v0, /device:TPU:4, one launch (start us, length us, event | category | flops | bytes accessed | tf_op | source)
XLA Modules:
  0.0 1084.3 jit_solution(14910961055857017236)
XLA Ops:
  7.2 0.8 fusion.72
  8.0 2.0 collective-permute-start
  10.1 7.4 collective-permute-start.1
  17.5 1.3 collective-permute-done.1
  18.8 0.7 pad_maximum_fusion.13
  19.6 3.1 collective-permute-start.2
  22.7 1.3 collective-permute-start.3
  24.2 4.4 collective-permute-done.3
  29.1 1.9 collective-permute-start.4
  31.0 7.3 collective-permute-start.5
  38.3 1.9 collective-permute-done.5
  40.2 1.3 collective-permute-start.6
  41.5 5.4 collective-permute-start.7
  46.9 1.3 collective-permute-done.7
  48.3 1.7 broadcast_multiply_fusion.2
  50.1 1.9 collective-permute-start.8
  52.0 7.3 collective-permute-start.9
  59.3 1.9 collective-permute-done.9
  61.2 1.3 collective-permute-start.10
  62.5 5.4 collective-permute-start.11
  67.9 1.3 collective-permute-done.11
  69.3 1.7 broadcast_multiply_fusion.1
  71.0 1.9 collective-permute-start.12
  73.0 7.3 collective-permute-start.13
  80.2 1.9 collective-permute-done.13
  82.1 1.3 collective-permute-start.14
  83.4 5.7 collective-permute-start.15
  89.2 1.3 collective-permute-done.15
  90.6 1.7 broadcast_multiply_fusion
  92.3 1.9 collective-permute-start.16
  94.3 7.3 collective-permute-start.17
  101.5 1.9 collective-permute-done.17
  103.4 1.3 collective-permute-start.18
  104.7 5.7 collective-permute-start.19
  110.5 1.3 collective-permute-done.19
  111.9 1.7 fusion.14
  113.6 1.6 convolution_bitcast_fusion.1
  115.5 453.4 %all-reduce.3.cloned.1.call-done = f32[128,128]{0,1:T(8,128)} async-done(((f32[128,128]{0,1:T(8,128)}), f32[128,128]{0,1:T(8,128)}) %all-reduce.3.cloned.1.call-update) | async-done | bytes 65552 | tf_op jit(solution)/shard_map/psum | solution.py:80
  568.9 1.0 copy.12
  569.9 11.7 %cholesky.14 = f32[128,128]{1,0:T(8,128)S(1)} custom-call(f32[128,128]{1,0:T(8,128)S(1)} %fusion.63), custom_call_target="Cholesky" | custom-call | tf_op jit(solution)/shard_map/jit(cholesky)/cholesky | solution.py:46
  581.6 0.6 compare_reduce_fusion
  582.3 0.7 fusion.61
  582.9 9.8 custom-call.7
  594.3 23.2 %while.26 = (s32[]{:T(128)}, f32[8,128,128]{2,1,0:T(8,128)}, f32[8,128]{1,0:T(8,128)S(1)}, s32[8,128]{1,0:T(8,128)S(1)}, s32[8]{0:T(128)S(1)}, /*index=5*/f32[10...) while((s32[]{:T(128)}, f32[8,128,128]{2,1,0:T(8,128)}, f32[8,128]{1,0:T(8,128)S(1)}, ...), condition=%wide.region_5.6_spmd, body=%wide.region_3.5_spmd.sunk | while | flops 201850880 | bytes 601725 | solution.py:98
  595.6 1.4 fusion.88
  598.5 1.4 fusion.88
  601.4 1.4 fusion.88
  604.3 1.4 fusion.88
  607.2 1.4 fusion.88
  610.1 1.4 fusion.88
  613.0 1.4 fusion.88
  615.9 1.4 fusion.88
  617.6 101.1 %psum.23 = f32[1024]{0:T(1024)S(1)} all-reduce(f32[1024]{0:T(1024)S(1)} %bitcast.54), channel_id=1, replica_groups=mesh['gy'=16,'gx'=32] {'gy','gx'}, use_global_device_ids=true, to_apply=%region_7.8 | all-reduce | flops 1024 | bytes 8192 | tf_op jit(solution)/shard_map/psum | solution.py:101
  718.7 350.4 %all-reduce.5.cloned.1.call-done = f32[1024,128]{1,0:T(8,128)} async-done(((f32[1024,128]{1,0:T(8,128)}), f32[1024,128]{1,0:T(8,128)}) %all-reduce.5.cloned.1.call-update) | async-done | bytes 524304 | tf_op jit(solution)/shard_map/psum | solution.py:101
  1069.0 1.2 broadcast_divide_fusion
  1070.3 6.3 while.27
  1070.4 0.6 fusion.92
  1071.2 0.6 fusion.92
  1072.0 0.6 fusion.92
  1072.8 0.6 fusion.92
  1073.6 0.6 fusion.92
  1074.4 0.6 fusion.92
  1076.0 0.6 fusion.92
  1076.7 0.8 copy-done.1
  (101 shorter events, 11.4 us)
Async XLA Ops:
  7.2 561.7 %all-reduce.3.cloned.1.call-start = ((), (), s32[]{:S(2)}) async-start(), calls=%async_computation | async-start | bytes 131072 | tf_op jit(solution)/shard_map/psum | solution.py:80
  8.0 20.6 %copy-start.5 = (f32[4,8,128]{2,1,0:T(8,128)S(1)}, f32[4,8,128]{2,1,0:T(8,128)}, u32[]{:S(2)}) copy-start(f32[4,8,128]{2,1,0:T(8,128)} %param.8) | copy-start | bytes 49156
  8.0 9.5 collective-permute-start
  10.1 18.8 %copy-start = (bf16[8,128,128]{2,1,0:T(8,128)(2,1)S(1)}, bf16[8,128,128]{2,1,0:T(8,128)(2,1)}, u32[]{:S(2)}) copy-start(bf16[8,128,128]{2,1,0:T(8,128)(2,1)} %param.7) | copy-start | bytes 786436
  10.1 8.7 collective-permute-start.1
  19.6 4.7 collective-permute-start.2
  22.7 6.0 collective-permute-start.3
  29.1 9.2 collective-permute-start.4
  31.0 9.1 collective-permute-start.5
  40.2 6.8 collective-permute-start.6
  41.5 6.8 collective-permute-start.7
  50.1 9.2 collective-permute-start.8
  52.0 9.1 collective-permute-start.9
  61.2 6.8 collective-permute-start.10
  62.5 6.8 collective-permute-start.11
  71.0 9.2 collective-permute-start.12
  73.0 9.1 collective-permute-start.13
  82.1 7.0 collective-permute-start.14
  83.4 7.0 collective-permute-start.15
  92.3 9.2 collective-permute-start.16
  94.3 9.1 collective-permute-start.17
  103.4 7.0 collective-permute-start.18
  104.7 7.0 collective-permute-start.19
  115.2 953.8 %all-reduce.5.cloned.1.call-start = ((), (), s32[]{:S(2)}) async-start(), calls=%async_computation.1 | async-start | bytes 1048576 | tf_op jit(solution)/shard_map/psum | solution.py:101
  568.8 1.0 copy-start.3
  593.6 0.7 copy-start.2
  1076.6 0.8 copy-start.1
  1076.7 0.8 copy-start.4
Sparse Core Ops, SparseCore 0:
  115.3 453.4 all-reduce.2
  617.7 451.3 all-reduce.4
where the time goes:
time: 1090 us; the launch traced here: 1080 us
  waiting for transfers between devices  823 us (76%)
  blocking collectives  101 us (9%)
  starting transfers between devices  78.3 us (7%)
  other arithmetic  35.1 us (3%)
  matrix products  18.7 us (2%)
  between operations  14.5 us (1%)
    psum x1, waiting for transfers between devices, on_device(): gram = lax.psum(gram_local, ('gy', 'gx'))  453 us
    psum x1, waiting for transfers between devices, on_device(): sums, counts = lax.psum((local_sums, local_counts), ('gy', 'gx'))  350 us
    psum x1, blocking collectives, on_device(): sums, counts = lax.psum((local_sums, local_counts), ('gy', 'gx'))  101 us
    ppermute x10, starting transfers between devices, extended(): lax.ppermute(lax.slice_in_dim(block, 0, width, axis=dim), axis, backward)  42.9 us
    ppermute x10, starting transfers between devices, extended(): lax.ppermute(lax.slice_in_dim(block, block.shape[dim] - width, None, axis...  35.1 us
  transfers between devices with their start and end apart: 22, of which 13 were waited for; matrix products, arithmetic and copies ran while one was open for 0% of the time, Pallas kernels for 0%

commit v1 on v0

--- a/solution.py
+++ b/solution.py
@@ -77,7 +77,7 @@
     gram_local = lax.dot_general(
         flat, flat, (((0,), (0,)), ((), ())), precision=highest, preferred_element_type=jnp.float32
     )
-    gram = lax.psum(gram_local, ("gy", "gx"))
+    gram = lax.all_gather(gram_local, axis_name=("gy", "gx")).sum(axis=0)
     transform = whitening(gram, total_pixels)
     whitened = jnp.dot(flat, transform, precision=highest, preferred_element_type=jnp.float32)
 

time: 1090 us -> 2130 us (1.95)
  waiting for transfers between devices: 823 us -> 1840 us
    all_gather x0 -> x1, waiting for transfers between devices: none -> 1470 us  [on_device(): gram = lax.all_gather(gram_local, axis_name=('gy', 'gx')).sum(axis=0)]
    psum x1 -> x0, waiting for transfers between devices: 453 us -> none  [on_device(): gram = lax.psum(gram_local, ('gy', 'gx'))]
where the time goes in v1:
time: 2130 us
  waiting for transfers between devices  1840 us (86%)
  blocking collectives  110 us (5%)
  starting transfers between devices  78 us (4%)
  other arithmetic  52.4 us (2%)
    all_gather x1, waiting for transfers between devices, on_device(): gram = lax.all_gather(gram_local, axis_name=('gy', 'gx')).sum(axis=0)  1470 us
    psum x1, waiting for transfers between devices, on_device(): sums, counts = lax.psum((local_sums, local_counts), ('gy', 'gx'))  355 us
    psum x1, blocking collectives, on_device(): sums, counts = lax.psum((local_sums, local_counts), ('gy', 'gx'))  110 us
    ppermute x10, starting transfers between devices, extended(): lax.ppermute(lax.slice_in_dim(block, 0, width, axis=dim), axis, backward)  42.7 us
  transfers between devices with their start and end apart: 22, of which 13 were waited for; matrix products, arithmetic and copies ran while one was open for 0% of the time, Pallas kernels for 0%

profile of v1, /device:TPU:4, one launch (start us, length us, event | category | flops | bytes accessed | tf_op | source)
XLA Modules:
  0.0 2130.6 jit_solution(1593534954685747406)
XLA Ops:
  7.2 0.8 fusion.72
  8.0 1.9 collective-permute-start
  9.9 7.3 collective-permute-start.1
  17.2 1.3 collective-permute-done.1
  18.5 0.7 pad_maximum_fusion.13
  19.3 3.1 collective-permute-start.2
  22.4 1.3 collective-permute-start.3
  24.0 4.4 collective-permute-done.3
  28.4 0.8 pad_maximum_fusion.12
  29.3 1.2 convert_multiply_fusion
  30.5 1.9 collective-permute-start.4
  32.4 7.3 collective-permute-start.5
  39.7 1.9 collective-permute-done.5
  41.6 1.3 collective-permute-start.6
  42.9 5.4 collective-permute-start.7
  48.3 1.3 collective-permute-done.7
  49.7 1.7 broadcast_multiply_fusion.2
  51.5 1.9 collective-permute-start.8
  53.4 7.3 collective-permute-start.9
  60.7 1.9 collective-permute-done.9
  62.5 1.3 collective-permute-start.10
  63.8 5.4 collective-permute-start.11
  69.3 1.3 collective-permute-done.11
  70.7 3.0 broadcast_multiply_fusion.1
  73.7 1.9 collective-permute-start.12
  75.6 7.3 collective-permute-start.13
  82.9 1.9 collective-permute-done.13
  84.8 1.3 collective-permute-start.14
  86.1 5.7 collective-permute-start.15
  91.8 1.3 collective-permute-done.15
  93.2 1.7 broadcast_multiply_fusion
  95.0 1.9 collective-permute-start.16
  96.9 7.3 collective-permute-start.17
  104.2 1.9 collective-permute-done.17
  106.1 1.3 collective-permute-start.18
  107.4 5.7 collective-permute-start.19
  113.1 1.3 collective-permute-done.19
  114.5 3.0 fusion.14
  117.5 1.6 convolution_bitcast_fusion.1
  119.4 1470.5 %all-gather.3.cloned.1.call-done = f32[65536,128]{1,0:T(8,128)} async-done(((f32[128,128]{1,0:T(8,128)}), f32[65536,128]{1,0:T(8,128)}) %all-gather.3.cloned.1.call-update) | async-done | bytes 33554448 | tf_op jit(solution)/shard_map/all_gather | solution.py:80
  1589.9 13.1 reduce_sum.40
  1603.1 11.7 cholesky.14
  1614.9 0.6 compare_reduce_fusion
  1615.5 0.7 fusion.61
  1616.2 9.8 custom-call.7
  1627.1 23.2 %while.26 = (s32[]{:T(128)}, f32[8,128,128]{2,1,0:T(8,128)}, f32[8,128]{1,0:T(8,128)S(1)}, s32[8,128]{1,0:T(8,128)S(1)}, s32[8]{0:T(128)S(1)}, /*index=5*/f32[10...) while((s32[]{:T(128)}, f32[8,128,128]{2,1,0:T(8,128)}, f32[8,128]{1,0:T(8,128)S(1)}, ...), condition=%wide.region_5.6_spmd, body=%wide.region_3.5_spmd.sunk | while | flops 201850880 | bytes 601725 | solution.py:98
  1628.3 1.4 fusion.88
  1631.2 1.4 fusion.88
  1634.1 1.4 fusion.88
  1637.0 1.4 fusion.88
  1639.9 1.4 fusion.88
  1642.8 1.4 fusion.88
  1645.7 1.4 fusion.88
  1648.6 1.4 fusion.88
  1650.3 110.5 %psum.15 = f32[1024]{0:T(1024)S(1)} all-reduce(f32[1024]{0:T(1024)S(1)} %bitcast.56), channel_id=1, replica_groups=mesh['gy'=16,'gx'=32] {'gy','gx'}, use_global_device_ids=true, to_apply=%region_7.8 | all-reduce | flops 1024 | bytes 8192 | tf_op jit(solution)/shard_map/psum | solution.py:101
  1760.8 354.5 %all-reduce.2.cloned.1.call-done = f32[1024,128]{1,0:T(8,128)} async-done(((f32[1024,128]{1,0:T(8,128)}), f32[1024,128]{1,0:T(8,128)}) %all-reduce.2.cloned.1.call-update) | async-done | bytes 524304 | tf_op jit(solution)/shard_map/psum | solution.py:101
  2115.3 1.2 broadcast_divide_fusion
  2116.6 6.4 while.27
  2116.7 0.6 fusion.92
  2117.5 0.6 fusion.92
  2119.1 0.6 fusion.92
  2119.9 0.6 fusion.92
  2121.5 0.6 fusion.92
  2123.0 0.8 copy-done
  (96 shorter events, 12.0 us)
Async XLA Ops:
  7.2 1582.7 %all-gather.3.cloned.1.call-start = ((), (), s32[]{:S(2)}) async-start(), calls=%async_computation.1 | async-start | bytes 33619968 | tf_op jit(solution)/shard_map/all_gather | solution.py:80
  8.0 9.2 collective-permute-start
  9.9 8.6 collective-permute-start.1
  19.3 4.7 collective-permute-start.2
  22.4 6.0 collective-permute-start.3
  30.5 9.2 collective-permute-start.4
  32.4 9.1 collective-permute-start.5
  41.6 6.8 collective-permute-start.6
  42.9 6.8 collective-permute-start.7
  49.7 1577.3 %copy-start.1 = (s32[8,128]{1,0:T(8,128)S(1)}, s32[8,128]{1,0:T(8,128)}, u32[]{:S(2)}) copy-start(s32[8,128]{1,0:T(8,128)} %param.9) | copy-start | bytes 12292
  51.5 9.2 collective-permute-start.8
  53.4 9.1 collective-permute-start.9
  62.5 6.8 collective-permute-start.10
  63.8 6.8 collective-permute-start.11
  73.7 9.2 collective-permute-start.12
  75.6 9.1 collective-permute-start.13
  84.8 7.0 collective-permute-start.14
  86.1 7.0 collective-permute-start.15
  95.0 9.2 collective-permute-start.16
  96.9 9.1 collective-permute-start.17
  106.1 7.0 collective-permute-start.18
  107.4 7.0 collective-permute-start.19
  119.2 1996.2 %all-reduce.2.cloned.1.call-start = ((), (), s32[]{:S(2)}) async-start(), calls=%async_computation | async-start | bytes 1048576 | tf_op jit(solution)/shard_map/psum | solution.py:101
  2123.0 0.8 copy-start
  2123.0 0.8 copy-start.2
Sparse Core Ops, SparseCore 0:
  119.3 1470.5 all-gather.2
  1650.4 464.8 all-reduce.1
